TPU v7x, 32 devices: a whole 2x2x4 slice. The times are simulated.
32 devices in a mesh: dp: 2 (over x), expert: 8 (over z, y), tensor: 2 (over core).
Axes of the slice: x: 2, y: 2, z: 4, core: 2. Of those that a mesh axis runs over, the one named last changes fastest.
Arguments:
- activations: bfloat16 [4096, 1536], P(('dp', 'expert', 'tensor')), may hold values from -6 to 6
- segments: int32 [16, 256], P(('dp', 'expert')), may hold values from 0 to 3, never falling along the last dimension, each value on 1 to 128 neighbouring positions
- routes: int32 [4096, 8], P(('dp', 'expert', 'tensor')), may hold values from 0 to 15, all different within a row; in each aligned block of 128 rows (0 to 127, 128 to 255, ...) at most 128 rows name the same one
- route_weights: float32 [4096, 8], P(('dp', 'expert', 'tensor')), may hold values from 0.03 to 0.3
- norm_attn_gain: float32 [1536], replicated, may hold values from 0.5 to 1.5
- norm_ffn_gain: float32 [1536], replicated, may hold values from 0.5 to 1.5
- query_weight: bfloat16 [1536, 1536], P(None, 'tensor'), may hold values from -0.15625 to 0.15625
- key_matrix: bfloat16 [1536, 512], P(None, 'tensor'), may hold values from -0.15625 to 0.15625
- value_matrix: bfloat16 [1536, 512], P(None, 'tensor'), may hold values from -0.15625 to 0.15625
- output_projection_weight: bfloat16 [1536, 1536], P('tensor'), may hold values from -0.625 to 0.625
- expert_gate: bfloat16 [16, 1536, 512], P('expert', None, 'tensor'), may hold values from -0.15625 to 0.15625
- expert_up: bfloat16 [16, 1536, 512], P('expert', None, 'tensor'), may hold values from -0.15625 to 0.15625
- expert_down: bfloat16 [16, 512, 1536], P('expert', 'tensor'), may hold values from -0.5 to 0.5
- grad_output: bfloat16 [4096, 1536], P(('dp', 'expert', 'tensor')), may hold values from -6 to 6
Outputs:
- block_out: bfloat16 [4096, 1536], P(('dp', 'expert', 'tensor'))
- grad_input: float32 [4096, 1536], P(('dp', 'expert', 'tensor'))
- grad_norm_attn: float32 [1536], replicated
- grad_norm_ffn: float32 [1536], replicated
- grad_query: float32 [1536, 1536], P(None, 'tensor')
- grad_key: float32 [1536, 512], P(None, 'tensor')
- grad_value: float32 [1536, 512], P(None, 'tensor')
- grad_mixer: float32 [1536, 1536], P('tensor')
- grad_expert_gate: float32 [16, 1536, 512], P('expert', None, 'tensor')
- grad_expert_up: float32 [16, 1536, 512], P('expert', None, 'tensor')
- grad_expert_down: float32 [16, 512, 1536], P('expert', 'tensor')
Inputs may be any that keep to these rules, and one draw needn't show every extreme that they name: `routes`: each row names 8 different experts; in the rows of one device (aligned blocks of 128 rows) no expert is named more than 128 times, and one is named exactly 128 times in some block. `segments`: each sequence's numbers never fall; 4 documents of 1 to 128 positions, one of exactly 128.
All inputs are finite; a program needn't handle non-finite values.
Results may differ from a plain program's by a relative error of at most 0.01.
Values may be sent and summed in bfloat16 or wider, within the bound.
No kernel may reach another device: no remote copies, remote signals or barrier semaphores. Data moves between devices by JAX's collectives and lax.ppermute only.
A program may use at most 320 MiB of HBM per device.

v0:
```python
import jax
import jax.numpy as jnp
from jax import lax
from jax.sharding import PartitionSpec as P

HEAD_DIM = 64
EPS = 1e-05
ATTN_SCALE = 0.015625
THETA = 10000.0
NEG_FILL = -1e30
F32 = jnp.float32
BF16 = jnp.bfloat16


def swap(values):
    return lax.ppermute(values, "tensor", [(0, 1), (1, 0)])


def norm_forward(values, gain_vector):
    inv_scale = lax.rsqrt(jnp.mean(values * values, axis=-1, keepdims=True) + EPS)
    return (values * inv_scale * gain_vector, inv_scale)


def norm_backward(values, inv_scale, gain_vector, upstream):
    weighted = upstream * gain_vector
    inner = jnp.mean(weighted * values, axis=-1, keepdims=True)
    value_gradient = inv_scale * weighted - values * (inv_scale * inv_scale * inv_scale) * inner
    grad_gain = jnp.sum(upstream * values * inv_scale, axis=0)
    return (value_gradient, grad_gain)


def rope_tables(position):
    frequency = THETA ** (-jnp.arange(HEAD_DIM // 2, dtype=F32) * 2.0 / HEAD_DIM)
    angle_table = position.astype(F32)[:, None] * frequency[None, :]
    return (jnp.cos(angle_table)[:, None, :], jnp.sin(angle_table)[:, None, :])


def rotate(field_in, cosine, sine):
    first, second = jnp.split(field_in, 2, axis=-1)
    return jnp.concatenate(
        [first * cosine - second * sine, second * cosine + first * sine], axis=-1
    )


def dot(spec, left, right):
    return jnp.einsum(spec, left, right, preferred_element_type=F32)


def body(
    activations,
    segments,
    routes,
    route_weights,
    norm_attn_gain,
    norm_ffn_gain,
    query_weight,
    key_matrix,
    value_matrix,
    output_projection_weight,
    expert_gate,
    expert_up,
    expert_down,
    grad_output,
):
    tensor_rank = lax.axis_index("tensor")
    rows, width = activations.shape
    experts_here = expert_gate.shape[0]
    expert_count = experts_here * lax.axis_size("expert")
    length = segments.shape[1]
    heads_q = query_weight.shape[1] // HEAD_DIM
    heads_kv = key_matrix.shape[1] // HEAD_DIM
    group = heads_q // heads_kv
    position = (jnp.arange(length, dtype=jnp.int32) + tensor_rank * rows) % length
    seg_ids = jnp.where(tensor_rank == 0, segments[0], jnp.roll(segments[0], rows))
    cosine, sine = rope_tables(position)
    allowed = (position[None, :] <= position[:, None]) & (seg_ids[None, :] == seg_ids[:, None])
    gate = jnp.concatenate([expert_gate, swap(expert_gate)], axis=2)
    up = jnp.concatenate([expert_up, swap(expert_up)], axis=2)
    down = jnp.concatenate([expert_down, swap(expert_down)], axis=1)
    upstream_all = lax.all_gather(grad_output, "expert", axis=0, tiled=True)
    named = routes[:, :, None] == jnp.arange(expert_count, dtype=jnp.int32)
    weight_table = jnp.sum(jnp.where(named, route_weights[:, :, None], 0.0), axis=1)
    weights_all = lax.all_gather(weight_table, "expert", axis=0, tiled=True)
    first_expert = lax.axis_index("expert") * experts_here
    weights_here = lax.dynamic_slice_in_dim(weights_all, first_expert, experts_here, 1).T
    x_in = jnp.concatenate([activations, swap(activations)], axis=0).astype(F32)
    normed_one, scale_one = norm_forward(x_in, norm_attn_gain)
    hidden_first = normed_one.astype(BF16)
    queries = dot("td,da->ta", hidden_first, query_weight).reshape(length, heads_q, HEAD_DIM)
    queries = rotate(queries, cosine, sine).astype(BF16).reshape(length, heads_kv, group, HEAD_DIM)
    keys = dot("td,da->ta", hidden_first, key_matrix).reshape(length, heads_kv, HEAD_DIM)
    keys = rotate(keys, cosine, sine).astype(BF16)
    value_rows = dot("td,da->ta", hidden_first, value_matrix).astype(BF16)
    value_rows = value_rows.reshape(length, heads_kv, HEAD_DIM)
    scores = jnp.where(allowed, dot("qhgd,khd->hgqk", queries, keys) * ATTN_SCALE, NEG_FILL)
    top_score = jnp.max(scores, axis=-1, keepdims=True)
    log_total = top_score + jnp.log(jnp.sum(jnp.exp(scores - top_score), axis=-1, keepdims=True))
    mixed = dot("hgqk,khd->qhgd", jnp.exp(scores - log_total).astype(BF16), value_rows).astype(BF16)
    mixed_flat = mixed.reshape(length, heads_q * HEAD_DIM)
    attn_part = dot("ta,ad->td", mixed_flat, output_projection_weight)
    residual = x_in[:rows] + attn_part[:rows] + swap(attn_part[rows:])
    normed_two, scale_two = norm_forward(residual, norm_ffn_gain)
    tokens_in = lax.all_gather(normed_two.astype(BF16), "expert", axis=0, tiled=True)
    pre_gate = dot("td,edf->etf", tokens_in, gate)
    pre_up = dot("td,edf->etf", tokens_in, up)
    gate_sigmoid = jax.nn.sigmoid(pre_gate)
    activated = (pre_gate * gate_sigmoid * pre_up).astype(BF16)
    expert_out = dot("etf,efd->etd", activated, down).astype(BF16)
    mix_part = jnp.sum(weights_here[:, :, None] * expert_out.astype(F32), axis=0).astype(BF16)
    grad_rows = (weights_here[:, :, None] * upstream_all.astype(F32)[None]).astype(BF16)
    grad_act = dot("etd,efd->etf", grad_rows, down)
    grad_pre_gate = (
        grad_act * pre_up * gate_sigmoid * (1.0 + pre_gate * (1.0 - gate_sigmoid))
    ).astype(BF16)
    grad_pre_up = (grad_act * pre_gate * gate_sigmoid).astype(BF16)
    grad_in = dot("etf,edf->etd", grad_pre_gate, gate) + dot("etf,edf->etd", grad_pre_up, up)
    grad_part = jnp.sum(weights_here[:, :, None] * grad_in, axis=0).astype(BF16)
    grad_h_own = lax.psum_scatter(grad_part, "expert", scatter_dimension=0, tiled=True)
    expert_mix = lax.psum_scatter(mix_part, "expert", scatter_dimension=0, tiled=True)
    block_out = (residual + expert_mix.astype(F32)).astype(BF16)

    def expert_sum(whole, axis):
        own, other = jnp.split(whole, 2, axis=axis)
        half = own + swap(other.astype(BF16)).astype(F32)
        return lax.psum(half.astype(BF16), "dp").astype(F32)

    gate_sum = expert_sum(dot("td,etf->edf", tokens_in, grad_pre_gate), 2)
    up_sum = expert_sum(dot("td,etf->edf", tokens_in, grad_pre_up), 2)
    down_sum = expert_sum(dot("etf,etd->efd", activated, grad_rows), 1)
    upstream_own = grad_output.astype(F32)
    grad_norm_part, grad_ffn_gain = norm_backward(
        residual, scale_two, norm_ffn_gain, grad_h_own.astype(F32)
    )
    grad_resid = upstream_own + grad_norm_part
    resid_own = grad_resid.astype(BF16)
    resid_full = jnp.concatenate([resid_own, swap(resid_own)], axis=0)
    grad_mix_w = dot("sa,sb->ab", mixed_flat, resid_full)
    mixed_grad = dot("im,dm->id", resid_full, output_projection_weight).astype(BF16)
    mixed_grad = mixed_grad.reshape(length, heads_kv, group, HEAD_DIM)
    probs = jnp.exp(scores - log_total)
    row_delta = dot("qhgd,qhgd->hgq", mixed_grad, mixed)
    grad_soft = dot("qhgd,khd->hgqk", mixed_grad, value_rows)
    grad_scores = (probs * (grad_soft - row_delta[..., None]) * ATTN_SCALE).astype(BF16)
    grad_queries = dot("hgqk,khd->qhgd", grad_scores, keys)
    grad_keys = dot("hgqk,qhgd->khd", grad_scores, queries)
    grad_values = dot("hgqk,qhgd->khd", probs.astype(BF16), mixed_grad)
    grad_q_rows = rotate(grad_queries.reshape(length, heads_q, HEAD_DIM), cosine, -sine)
    grad_q_rows = grad_q_rows.astype(BF16).reshape(length, -1)
    grad_k_rows = rotate(grad_keys, cosine, -sine).astype(BF16).reshape(length, -1)
    grad_v_rows = grad_values.astype(BF16).reshape(length, -1)
    grad_q_w = dot("sd,sa->da", hidden_first, grad_q_rows)
    grad_k_w = dot("sd,sa->da", hidden_first, grad_k_rows)
    grad_v_w = dot("sd,sa->da", hidden_first, grad_v_rows)
    grad_h_part = (
        dot("sa,da->sd", grad_q_rows, query_weight)
        + dot("sa,da->sd", grad_k_rows, key_matrix)
        + dot("sa,da->sd", grad_v_rows, value_matrix)
    )
    grad_h_one = grad_h_part[:rows] + swap(grad_h_part[rows:])
    grad_x_part, grad_attn_gain = norm_backward(
        x_in[:rows], scale_one[:rows], norm_attn_gain, grad_h_one
    )
    grad_input = grad_resid + grad_x_part
    dense = [t.astype(BF16) for t in (grad_q_w, grad_k_w, grad_v_w, grad_mix_w)]
    dense = [t.astype(F32) for t in lax.psum(dense, ("dp", "expert"))]
    gains = lax.psum(jnp.stack([grad_attn_gain, grad_ffn_gain]), ("dp", "expert", "tensor"))
    return (block_out, grad_input, gains[0], gains[1], *dense, gate_sum, up_sum, down_sum)


def solution(mesh):
    tokens = P(("dp", "expert", "tensor"), None)
    whole = P()
    columns = P(None, "tensor")
    hidden_last = P("expert", None, "tensor")
    hidden_mid = P("expert", "tensor", None)
    mixer = P("tensor", None)
    return jax.shard_map(
        body,
        mesh=mesh,
        in_specs=(
            tokens,
            P(("dp", "expert"), None),
            tokens,
            tokens,
            whole,
            whole,
            columns,
            columns,
            columns,
            mixer,
            hidden_last,
            hidden_last,
            hidden_mid,
            tokens,
        ),
        out_specs=(
            tokens,
            tokens,
            whole,
            whole,
            columns,
            columns,
            columns,
            mixer,
            hidden_last,
            hidden_last,
            hidden_mid,
        ),
        check_vma=False,
    )
```

profile of v0, /device:TPU:0, one launch (start us, length us, event | category | flops | bytes accessed | tf_op | source)
XLA Modules:
  0.0 691.7 jit_solution(6405158610316332684)
XLA Ops:
  26.6 2.6 copy.79
  29.6 2.6 copy.77
  32.3 32.2 %all_gather.9 = f32[1024,16]{0,1:T(8,128)S(1)} all-gather(f32[128,16]{0,1:T(8,128)S(1)} %select_reduce_fusion), channel_id=1, replica_groups=mesh['dp'=2,'expert'=8,'tensor'=2] {'expert'}, dimensions={0}, use_global_device_ids=true | all-gather | bytes 73728 | tf_op jit(solution)/shard_map/all_gather | solution.py:83
  64.6 2.7 constant_dynamic-update-slice_fusion.1
  67.2 2.7 constant_dynamic-update-slice_fusion
  69.9 4.5 all-gather.5.cloned.1.call-done
  74.3 5.4 convert_element_type.165
  79.7 56.4 %all-gather.3.cloned.1.call-done = bf16[1024,1536]{1,0:T(8,128)(2,1)} async-done(((bf16[128,1536]{1,0:T(8,128)(2,1)}), bf16[1024,1536]{1,0:T(8,128)(2,1)}) %all-gather.3.cloned.1.call-update) | async-done | bytes 3145744 | tf_op jit(solution)/shard_map/all_gather | solution.py:103
  136.1 6.9 %fusion.24 = f32[2,512,1024]{2,1,0:T(8,128)S(1)} fusion(bf16[1024,1536]{1,0:T(8,128)(2,1)} %all-gather.3.cloned.1.call-done, bf16[2,1536,256]{1,2,0:T(8,128)(2,1)} %collective-permute-done.3, bf16[2,1536,256]{1,2,0:T(8,128)(2,1)} %copy.79), kind=kOutput, calls=%fused_computation.46 | convolution fusion | flops 3227516928 | bytes 10485760 | tf_op jit(solution)/shard_map/td,edf->etf/dot_general | solution.py:46
  143.1 6.5 fusion.26
  149.7 9.5 %fusion.9 = (bf16[2,1024,512]{1,2,0:T(8,128)(2,1)}, bf16[2,1024,512]{1,2,0:T(8,128)(2,1)}, bf16[2,1024,512]{1,2,0:T(8,128)(2,1)S(1)}) fusion(f32[2,512,1024]{2,1,0:T(8,128)S(1)} %fusion.24, f32[2,512,1024]{2,1,0:T(8,128)} %fusion.26, bf16[2,512,1536]{2,1,0:T(8,128)(2,1)} %constant_dynamic-update-slice_fusion, f32[1024,1536]{1,0:T(8,128)S(1)} %bitcast.160, ...), kind=kOutput, calls=%fused_computation.16 | convolution fusion | flops 3244294144 | bytes 24125440 | tf_op jit(solution)/shard_map/etd,efd->etf/dot_general | solution.py:46
  159.1 8.6 %fusion.30 = f32[2,1024,1536]{2,1,0:T(8,128)} fusion(bf16[2,1024,512]{1,2,0:T(8,128)(2,1)S(1)} %get-tuple-element.61, bf16[2,1536,256]{1,2,0:T(8,128)(2,1)} %collective-permute-done.3, bf16[2,1536,256]{1,2,0:T(8,128)(2,1)S(1)} %copy-done.11), kind=kOutput, calls=%fused_computation.59 | convolution fusion | flops 3227516928 | bytes 17825792 | tf_op jit(solution)/shard_map/etf,edf->etd/dot_general | solution.py:46
  167.7 13.0 %multiply_reduce_fusion = bf16[1024,1536]{1,0:T(8,128)(2,1)} fusion(f32[2,1024,1536]{2,1,0:T(8,128)} %fusion.30, f32[2,1024]{1,0:T(2,128)S(1)} %dynamic-slice_bitcast_fusion, bf16[2,1024,512]{1,2,0:T(8,128)(2,1)} %get-tuple-element.59, bf16[2,1536,256]{1,2,0:T(8,128)(2,1)} %collective-permute-done.2, bf16[2,1536,256]{1,2,0:T(8,128)(2,1)} %copy.77), kind=kOutput, calls=%fused_computation | convolution fusion | flops 3235381248 | bytes 20979712 | tf_op jit(solution)/shard_map/etf,edf->etd/dot_general | solution.py:46
  181.0 7.1 %fusion = f32[2,512,1536]{2,1,0:T(8,128)S(1)} fusion(bf16[2,1024,512]{1,2,0:T(8,128)(2,1)} %get-tuple-element.60, f32[1024,1536]{1,0:T(8,128)} %convert_element_type.165, f32[2,1024]{1,0:T(2,128)S(1)} %dynamic-slice_bitcast_fusion), kind=kOutput, calls=%fused_computation.3 | convolution fusion | flops 3227516928 | bytes 14688256 | tf_op jit(solution)/shard_map/etf,etd->efd/dot_general | solution.py:46
  190.0 3.4 convolution_bitcast_fusion.1
  195.0 3.4 convolution_bitcast_fusion
  203.8 8.9 %multiply_reduce_fusion.1 = bf16[1024,1536]{1,0:T(8,128)(2,1)} fusion(f32[2,1024]{1,0:T(2,128)S(1)} %dynamic-slice_bitcast_fusion, bf16[2,1024,512]{1,2,0:T(8,128)(2,1)} %get-tuple-element.60, bf16[2,512,1536]{2,1,0:T(8,128)(2,1)} %constant_dynamic-update-slice_fusion), kind=kOutput, calls=%fused_computation.2 | convolution fusion | flops 3232235520 | bytes 8396800 | tf_op jit(solution)/shard_map/etf,efd->etd/dot_general | solution.py:46
  212.9 41.2 %reduce-scatter.5.cloned.1.call-done = bf16[128,1536]{1,0:T(8,128)(2,1)} async-done(((bf16[1024,1536]{1,0:T(8,128)(2,1)}), bf16[128,1536]{1,0:T(8,128)(2,1)}) %reduce-scatter.5.cloned.1.call-update) | async-done | bytes 393232 | tf_op jit(solution)/shard_map/reduce_scatter | solution.py:118
  264.6 3.2 fusion.21
  276.0 2.3 convolution_convert_fusion.1
  279.3 2.6 fusion.68
  287.1 88.6 %all-reduce.7.cloned.1.call-done = (bf16[2,1536,256]{1,2,0:T(8,128)(2,1)}, bf16[2,1536,256]{1,2,0:T(8,128)(2,1)}, bf16[2,256,1536]{2,1,0:T(8,128)(2,1)}) async-done(((bf16[2,1536,256]{1,2,0:T(8,128)(2,1)}, bf16[2,1536,256]{1,2,0:T(8,128)(2,1)}, bf16[2,256,1536]{2,1,0:T(8,128)(2,1)}), (bf16[2,1536,256]{1,2,0:T(8,128)(2,1)}, bf16[2,1536,256]{1,2,0:T(8,128)(2,1)}, ...) | async-done | bytes 4718608 | tf_op jit(solution)/shard_map/psum | solution.py:125
  375.8 3.1 copy.91
  378.8 3.1 copy.92
  381.9 3.6 convert_element_type.194
  388.2 40.9 %psum.56 = f32[2,1536]{1,0:T(2,128)} all-reduce(f32[2,1536]{1,0:T(2,128)} %pad_maximum_fusion.14), channel_id=1, replica_groups=mesh['dp'=2,'expert'=8,'tensor'=2] {'dp','expert','tensor'}, use_global_device_ids=true, to_apply=%region_13.14 | all-reduce | flops 3072 | bytes 24576 | tf_op jit(solution)/shard_map/psum | solution.py:166
  431.6 24.1 %reduce-scatter.3.cloned.1.call-done = bf16[128,1536]{1,0:T(8,128)(2,1)} async-done(((bf16[1024,1536]{1,0:T(8,128)(2,1)}), bf16[128,1536]{1,0:T(8,128)(2,1)}) %reduce-scatter.3.cloned.1.call-update) | async-done | bytes 393232 | tf_op jit(solution)/shard_map/reduce_scatter | solution.py:119
  455.7 3.3 subtract_add_fusion
  459.0 216.4 %all-reduce.5.cloned.1.call-done = (bf16[1536,768]{1,0:T(8,128)(2,1)}, bf16[1536,256]{1,0:T(8,128)(2,1)}, bf16[1536,256]{1,0:T(8,128)(2,1)}, bf16[768,1536]{1,0:T(8,128)(2,1)}) async-done(((bf16[1536,768]{1,0:T(8,128)(2,1)}, bf16[1536,256]{1,0:T(8,128)(2,1)}, bf16[1536,256]{1,0:T(8,128)(2,1)}, bf16[768,1536]{1,0:T(8,128)(2,1)}), (bf16[1536,768]{1,0:T(8,128)(2,1)}, bf16[1536,256]{1,0:T(8,128)(2,1)}, ...) | async-done | bytes 6291472 | tf_op jit(solution)/shard_map/psum | solution.py:165
  675.5 2.5 convert_element_type.181
  679.3 2.5 convert_element_type.179
  681.8 2.8 convert_element_type.185
  (231 shorter events, 60.0 us)
Async XLA Ops:
  7.2 13.7 %copy-start = (bf16[768,1536]{1,0:T(8,128)(2,1)S(1)}, bf16[768,1536]{1,0:T(8,128)(2,1)}, u32[]{:S(2)}) copy-start(bf16[768,1536]{1,0:T(8,128)(2,1)} %param.23) | copy-start | bytes 7077892
  7.2 7.8 %copy-start.13 = (bf16[128,1536]{1,0:T(8,128)(2,1)S(1)}, bf16[128,1536]{1,0:T(8,128)(2,1)}, u32[]{:S(2)}) copy-start(bf16[128,1536]{1,0:T(8,128)(2,1)} %param.14) | copy-start | bytes 1179652
  7.2 7.8 %copy-start.46 = (f32[1536]{0:T(1024)S(1)}, f32[1536]{0:T(1024)}, u32[]{:S(2)}) copy-start(f32[1536]{0:T(1024)} %param.18) | copy-start | bytes 18436
  7.2 67.1 %all-gather.5.cloned.1.call-start = ((), (), s32[]{:S(2)}) async-start(), calls=%async_computation.4 | async-start | bytes 3538944 | tf_op jit(solution)/shard_map/all_gather | solution.py:80
  8.0 128.2 %all-gather.3.cloned.1.call-start = ((), (), s32[]{:S(2)}) async-start(), calls=%async_computation.2 | async-start | bytes 3538944 | tf_op jit(solution)/shard_map/all_gather | solution.py:103
  8.0 3.7 collective-permute-start
  10.9 9.1 %copy-start.41 = (pred[256,256]{0,1:T(8,128)(4,1)}, pred[256,256]{0,1:T(8,128)(4,1)S(1)}, u32[]{:S(2)}) copy-start(pred[256,256]{0,1:T(8,128)(4,1)S(1)} %compare_and_fusion) | copy-start | bytes 196612
  11.7 10.1 %copy-start.15 = (bf16[128,1536]{1,0:T(8,128)(2,1)}, bf16[128,1536]{1,0:T(8,128)(2,1)S(1)}, u32[]{:S(2)}) copy-start(bf16[128,1536]{1,0:T(8,128)(2,1)S(1)} %collective-permute-done) | copy-start | bytes 1179652
  21.8 2.4 collective-permute-start.1
  26.4 227.7 %reduce-scatter.5.cloned.1.call-start = ((), (), s32[]{:S(2)}) async-start(), calls=%async_computation.5 | async-start | bytes 3538944 | tf_op jit(solution)/shard_map/reduce_scatter | solution.py:118
  26.4 40.8 %collective-permute-start.4 = (bf16[2,256,1536]{2,1,0:T(8,128)(2,1)}, bf16[2,256,1536]{2,1,0:T(8,128)(2,1)}, u32[]{:S(2)}, u32[]{:S(2)}) collective-permute-start(bf16[2,256,1536]{2,1,0:T(8,128)(2,1)} %param.26), channel_id=1, source_target_pairs={{0,1},{1,0},{2,3},{3,2},{4,5},{5,4},{6,7},{7,6},{8,9},{9,8},{10,11... | collective-permute-start | bytes 4718600 | tf_op jit(solution)/shard_map/ppermute | solution.py:16
  29.2 50.5 %collective-permute-start.3 = (bf16[2,1536,256]{1,2,0:T(8,128)(2,1)}, bf16[2,1536,256]{1,2,0:T(8,128)(2,1)}, u32[]{:S(2)}, u32[]{:S(2)}) collective-permute-start(bf16[2,1536,256]{1,2,0:T(8,128)(2,1)} %copy.79), channel_id=1, source_target_pairs={{0,1},{1,0},{2,3},{3,2},{4,5},{5,4},{6,7},{7,6},{8,9},{9,8},{10,11... | collective-permute-start | bytes 4718600 | tf_op jit(solution)/shard_map/ppermute | solution.py:16
  32.2 110.9 %collective-permute-start.2 = (bf16[2,1536,256]{1,2,0:T(8,128)(2,1)}, bf16[2,1536,256]{1,2,0:T(8,128)(2,1)}, u32[]{:S(2)}, u32[]{:S(2)}) collective-permute-start(bf16[2,1536,256]{1,2,0:T(8,128)(2,1)} %copy.77), channel_id=1, source_target_pairs={{0,1},{1,0},{2,3},{3,2},{4,5},{5,4},{6,7},{7,6},{8,9},{9,8},{10,11... | collective-permute-start | bytes 4718600 | tf_op jit(solution)/shard_map/ppermute | solution.py:16
  136.1 7.0 %copy-start.12 = (bf16[2,1536,256]{1,2,0:T(8,128)(2,1)S(1)}, bf16[2,1536,256]{1,2,0:T(8,128)(2,1)}, u32[]{:S(2)}) copy-start(bf16[2,1536,256]{1,2,0:T(8,128)(2,1)} %copy.77) | copy-start | bytes 4718596
  136.1 7.0 %copy-start.61 = (bf16[1024,1536]{1,0:T(8,128)(2,1)S(1)}, bf16[1024,1536]{1,0:T(8,128)(2,1)}, u32[]{:S(2)}) copy-start(bf16[1024,1536]{1,0:T(8,128)(2,1)} %all-gather.3.cloned.1.call-done) | copy-start | bytes 9437188
  136.1 13.5 %slice-start = ((s8[6291456]{0:T(1024)(128)(4,1)}), s8[4194304]{0:T(1024)(128)(4,1)S(1)}, s32[]{:S(2)}) async-start(s8[6291456]{0:T(1024)(128)(4,1)} %bitcast.159), calls=%async_computation.8 | async-start | bytes 8388608
  143.1 6.6 slice-start.1
  149.6 9.5 %copy-start.11 = (bf16[2,1536,256]{1,2,0:T(8,128)(2,1)S(1)}, bf16[2,1536,256]{1,2,0:T(8,128)(2,1)}, u32[]{:S(2)}) copy-start(bf16[2,1536,256]{1,2,0:T(8,128)(2,1)} %copy.79) | copy-start | bytes 4718596
  159.1 8.6 %copy-start.64 = (bf16[2,1024,512]{1,2,0:T(8,128)(2,1)}, bf16[2,1024,512]{1,2,0:T(8,128)(2,1)S(1)}, u32[]{:S(2)}) copy-start(bf16[2,1024,512]{1,2,0:T(8,128)(2,1)S(1)} %get-tuple-element.61) | copy-start | bytes 6291460
  180.8 195.0 %all-reduce.7.cloned.1.call-start = ((), (), s32[]{:S(2)}) async-start(), calls=%async_computation.7 | async-start | bytes 9437184 | tf_op jit(solution)/shard_map/psum | solution.py:125
  181.0 7.3 %copy-start.66 = (bf16[2,1024,512]{1,2,0:T(8,128)(2,1)S(1)}, bf16[2,1024,512]{1,2,0:T(8,128)(2,1)}, u32[]{:S(2)}) copy-start(bf16[2,1024,512]{1,2,0:T(8,128)(2,1)} %get-tuple-element.59) | copy-start | bytes 6291460
  188.3 10.4 %collective-permute-start.9 = (bf16[2,256,1536]{2,1,0:T(8,128)(2,1)S(1)}, bf16[2,256,1536]{2,1,0:T(8,128)(2,1)S(1)}, u32[]{:S(2)}, u32[]{:S(2)}) collective-permute-start(bf16[2,256,1536]{2,1,0:T(8,128)(2,1)S(1)} %split.101), channel_id=1, source_target_pairs={{0,1},{1,0},{2,3},{3,2},{4,5},{5,4},{6,7},{7,6},{8,9},{9,8},{10,11... | collective-permute-start | bytes 4718600 | tf_op jit(solution)/shard_map/ppermute | solution.py:16
  193.6 6.7 collective-permute-start.7
  198.6 3.5 collective-permute-start.8
  203.7 252.0 %reduce-scatter.3.cloned.1.call-start = ((), (), s32[]{:S(2)}) async-start(), calls=%async_computation.3 | async-start | bytes 3538944 | tf_op jit(solution)/shard_map/reduce_scatter | solution.py:119
  212.6 41.5 %copy-start.52 = (f32[128]{0:T(128)S(1)}, f32[128]{0:T(128)}, u32[]{:S(2)}) copy-start(f32[128]{0:T(128)} %copy-done.51) | copy-start | bytes 1540
  212.6 43.3 %copy-start.56 = (f32[128]{0:T(128)S(1)}, f32[128]{0:T(128)}, u32[]{:S(2)}) copy-start(f32[128]{0:T(128)} %get-tuple-element.79) | copy-start | bytes 1540
  212.6 462.8 %all-reduce.5.cloned.1.call-start = ((), (), s32[]{:S(2)}) async-start(), calls=%async_computation.6 | async-start | bytes 12582912 | tf_op jit(solution)/shard_map/psum | solution.py:165
  257.4 1.8 collective-permute-start.5
  269.3 6.7 copy-start.18
  285.6 100.0 %collective-permute-start.6 = (f32[128,1536]{1,0:T(8,128)}, f32[128,1536]{1,0:T(8,128)}, u32[]{:S(2)}, u32[]{:S(2)}) collective-permute-start(f32[128,1536]{1,0:T(8,128)} %slice.53), channel_id=1, source_target_pairs={{0,1},{1,0},{2,3},{3,2},{4,5},{5,4},{6,7},{7,6},{8,9},{9,8},{10,11... | collective-permute-start | bytes 2359304 | tf_op jit(solution)/shard_map/ppermute | solution.py:16
  385.6 70.2 %copy-start.5 = (bf16[128,1536]{1,0:T(8,128)(2,1)S(1)}, bf16[128,1536]{1,0:T(8,128)(2,1)}, u32[]{:S(2)}) copy-start(bf16[128,1536]{1,0:T(8,128)(2,1)} %param.27) | copy-start | bytes 1179652
  (53 other events, 121.1 us)
Sparse Core Ops, SparseCore 0:
  10.2 64.0 all-gather.4
  77.1 58.9 all-gather.2
  180.9 73.1 reduce-scatter.4
  256.6 119.1 all-reduce.6
  380.2 75.4 reduce-scatter.2
  463.7 211.6 all-reduce.4
where the time goes:
time: 699 us; the launch traced here: 692 us
  waiting for transfers between devices  436 us (62%)
  matrix products  90.5 us (13%)
  blocking collectives  73.1 us (10%)
  other arithmetic  41.7 us (6%)
  local copies, waits for them, and re-layouts  32.8 us (5%)
  between operations  15.2 us (2%)
    psum x1, waiting for transfers between devices, body(): dense = [t.astype(F32) for t in lax.psum(dense, ('dp', 'expert'))]  216 us
    dot_general x27, matrix products, dot(): return jnp.einsum(spec, left, right, preferred_element_type=F32)  90.5 us
    psum x1, waiting for transfers between devices, expert_sum(): return lax.psum(half.astype(BF16), 'dp').astype(F32)  88.6 us
    all_gather x1, waiting for transfers between devices, body(): lax.all_gather(normed_two.astype(BF16), 'expert', axis=0, tiled=True)  56.4 us
    reduce_scatter x1, waiting for transfers between devices, body(): lax.psum_scatter(grad_part, 'expert', scatter_dimension=0, tiled=True)  41.2 us
    psum x1, blocking collectives, body(): lax.psum(jnp.stack([grad_attn_gain, grad_ffn_gain]), ('dp', 'expert', 'te...  40.9 us
    all_gather x1, blocking collectives, body(): weights_all = lax.all_gather(weight_table, 'expert', axis=0, tiled=True)  32.2 us
    reduce_scatter x1, waiting for transfers between devices, body(): lax.psum_scatter(mix_part, 'expert', scatter_dimension=0, tiled=True)  24.1 us
  transfers between devices with their start and end apart: 16, of which 8 were waited for; matrix products, arithmetic and copies ran while one was open for 16% of the time, Pallas kernels for 0%

commit v1 on v0

--- a/solution.py
+++ b/solution.py
@@ -77,10 +77,15 @@
     gate = jnp.concatenate([expert_gate, swap(expert_gate)], axis=2)
     up = jnp.concatenate([expert_up, swap(expert_up)], axis=2)
     down = jnp.concatenate([expert_down, swap(expert_down)], axis=1)
-    upstream_all = lax.all_gather(grad_output, "expert", axis=0, tiled=True)
     named = routes[:, :, None] == jnp.arange(expert_count, dtype=jnp.int32)
     weight_table = jnp.sum(jnp.where(named, route_weights[:, :, None], 0.0), axis=1)
-    weights_all = lax.all_gather(weight_table, "expert", axis=0, tiled=True)
+    upstream_all, weights_all = jnp.split(
+        lax.all_gather(
+            jnp.concatenate([grad_output, weight_table], axis=1), "expert", axis=0, tiled=True
+        ),
+        [grad_output.shape[1]],
+        axis=1,
+    )
     first_expert = lax.axis_index("expert") * experts_here
     weights_here = lax.dynamic_slice_in_dim(weights_all, first_expert, experts_here, 1).T
     x_in = jnp.concatenate([activations, swap(activations)], axis=0).astype(F32)

time: 699 us -> 753 us (1.077)
  waiting for transfers between devices: 436 us -> 512 us
  blocking collectives: 73.1 us -> 40.8 us
  local copies, waits for them, and re-layouts: 32.8 us -> 40.8 us
    all_gather x1, waiting for transfers between devices: 4.46 us -> 91.9 us  [body(): lax.all_gather(jnp.concatenate([grad_output, weight_table], axis=1), 'exp...]
    all_gather x1 -> x0, blocking collectives: 32.2 us -> none  [body(): weights_all = lax.all_gather(weight_table, 'expert', axis=0, tiled=True)]
    all_gather x1, waiting for transfers between devices: 56.4 us -> 46.7 us  [body(): lax.all_gather(normed_two.astype(BF16), 'expert', axis=0, tiled=True)]
    unnamed x143 -> x139, local copies, waits for them, and re-layouts: 23.8 us -> 24.5 us
  transfers between devices with their start and end apart: 16 -> 16, of which waited for: 8 -> 8; matrix products, arithmetic and copies ran while one was open for 16% -> 14% of each run, Pallas kernels for 0% -> 0%
where the time goes in v1:
time: 753 us; the launch traced here: 747 us
  waiting for transfers between devices  512 us (68%)
  matrix products  94.4 us (13%)
  local copies, waits for them, and re-layouts  40.8 us (5%)
  blocking collectives  40.8 us (5%)
  other arithmetic  39.9 us (5%)
  between operations  15.4 us (2%)
    psum x1, waiting for transfers between devices, body(): dense = [t.astype(F32) for t in lax.psum(dense, ('dp', 'expert'))]  216 us
    dot_general x27, matrix products, dot(): return jnp.einsum(spec, left, right, preferred_element_type=F32)  94.4 us
    all_gather x1, waiting for transfers between devices, body(): lax.all_gather(jnp.concatenate([grad_output, weight_table], axis=1), 'exp...  91.9 us
    psum x1, waiting for transfers between devices, expert_sum(): return lax.psum(half.astype(BF16), 'dp').astype(F32)  88.6 us
    all_gather x1, waiting for transfers between devices, body(): lax.all_gather(normed_two.astype(BF16), 'expert', axis=0, tiled=True)  46.7 us
    psum x1, blocking collectives, body(): lax.psum(jnp.stack([grad_attn_gain, grad_ffn_gain]), ('dp', 'expert', 'te...  40.8 us
    reduce_scatter x1, waiting for transfers between devices, body(): lax.psum_scatter(grad_part, 'expert', scatter_dimension=0, tiled=True)  40.6 us
    unnamed x139, local copies, waits for them, and re-layouts  24.5 us
  transfers between devices with their start and end apart: 16, of which 8 were waited for; matrix products, arithmetic and copies ran while one was open for 14% of the time, Pallas kernels for 0%

profile of v1, /device:TPU:0, one launch (start us, length us, event | category | flops | bytes accessed | tf_op | source)
XLA Modules:
  0.0 746.7 jit_solution(5621497385503620961)
XLA Ops:
  30.7 2.6 copy.83
  33.6 2.6 copy.81
  36.4 2.7 constant_dynamic-update-slice_fusion.1
  39.1 2.7 constant_dynamic-update-slice_fusion
  41.8 46.7 %all-gather.5.cloned.1.call-done = bf16[1024,1536]{1,0:T(8,128)(2,1)} async-done(((bf16[128,1536]{1,0:T(8,128)(2,1)}), bf16[1024,1536]{1,0:T(8,128)(2,1)}) %all-gather.5.cloned.1.call-update) | async-done | bytes 3145744 | tf_op jit(solution)/shard_map/all_gather | solution.py:108
  88.4 8.4 %fusion.24 = f32[2,512,1024]{2,1,0:T(8,128)} fusion(bf16[1024,1536]{1,0:T(8,128)(2,1)} %all-gather.5.cloned.1.call-done, bf16[2,1536,256]{1,2,0:T(8,128)(2,1)} %collective-permute-done.3, bf16[2,1536,256]{1,2,0:T(8,128)(2,1)} %copy.83), kind=kOutput, calls=%fused_computation.46 | convolution fusion | flops 3227516928 | bytes 10485760 | tf_op jit(solution)/shard_map/td,edf->etf/dot_general | solution.py:46
  96.9 6.6 fusion.26
  103.5 91.9 %all-gather.3.cloned.1.call-done = f32[1024,1552]{1,0:T(8,128)} async-done(((f32[128,1552]{1,0:T(8,128)}), f32[1024,1552]{1,0:T(8,128)}) %all-gather.3.cloned.1.call-update) | async-done | bytes 6357008 | tf_op jit(solution)/shard_map/all_gather | solution.py:83
  198.7 3.4 split.72
  202.7 11.6 %fusion.9 = (bf16[2,1024,512]{1,2,0:T(8,128)(2,1)}, bf16[2,1024,512]{1,2,0:T(8,128)(2,1)}, bf16[2,1024,512]{1,2,0:T(8,128)(2,1)S(1)}) fusion(f32[2,512,1024]{2,1,0:T(8,128)S(1)} %copy-done.66, f32[2,512,1024]{2,1,0:T(8,128)} %fusion.26, bf16[2,512,1536]{2,1,0:T(8,128)(2,1)} %constant_dynamic-update-slice_fusion, f32[1024,1536]{1,0:T(8,128)S(1)} %split.72, ...), kind=kOutput, calls=%fused_computation.16 | convolution fusion | flops 3244294144 | bytes 24125440 | tf_op jit(solution)/shard_map/etd,efd->etf/dot_general | solution.py:46
  214.4 8.7 %fusion.30 = f32[2,1024,1536]{2,1,0:T(8,128)} fusion(bf16[2,1024,512]{1,2,0:T(8,128)(2,1)S(1)} %get-tuple-element.61, bf16[2,1536,256]{1,2,0:T(8,128)(2,1)} %collective-permute-done.3, bf16[2,1536,256]{1,2,0:T(8,128)(2,1)S(1)} %copy-done.12), kind=kOutput, calls=%fused_computation.59 | convolution fusion | flops 3227516928 | bytes 17825792 | tf_op jit(solution)/shard_map/etf,edf->etd/dot_general | solution.py:46
  223.2 13.0 %multiply_reduce_fusion = bf16[1024,1536]{1,0:T(8,128)(2,1)} fusion(f32[2,1024,1536]{2,1,0:T(8,128)} %fusion.30, f32[2,1024]{1,0:T(2,128)S(1)} %copy.79, bf16[2,1024,512]{1,2,0:T(8,128)(2,1)} %get-tuple-element.59, bf16[2,1536,256]{1,2,0:T(8,128)(2,1)} %collective-permute-done.2, bf16[2,1536,256]{1,2,0:T(8,128)(2,1)} %copy.81), kind=kOutput, calls=%fused_computation | convolution fusion | flops 3235381248 | bytes 20979712 | tf_op jit(solution)/shard_map/etf,edf->etd/dot_general | solution.py:46
  236.5 7.1 fusion
  245.5 3.4 convolution_bitcast_fusion.1
  250.5 3.4 convolution_bitcast_fusion
  259.5 8.9 %multiply_reduce_fusion.1 = bf16[1024,1536]{1,0:T(8,128)(2,1)} fusion(f32[2,1024]{1,0:T(2,128)S(1)} %copy.79, bf16[2,1024,512]{1,2,0:T(8,128)(2,1)} %get-tuple-element.60, bf16[2,512,1536]{2,1,0:T(8,128)(2,1)} %constant_dynamic-update-slice_fusion), kind=kOutput, calls=%fused_computation.2 | convolution fusion | flops 3232235520 | bytes 8396800 | tf_op jit(solution)/shard_map/etf,efd->etd/dot_general | solution.py:46
  268.4 40.6 %reduce-scatter.5.cloned.1.call-done = bf16[128,1536]{1,0:T(8,128)(2,1)} async-done(((bf16[1024,1536]{1,0:T(8,128)(2,1)}), bf16[128,1536]{1,0:T(8,128)(2,1)}) %reduce-scatter.5.cloned.1.call-update) | async-done | bytes 393232 | tf_op jit(solution)/shard_map/reduce_scatter | solution.py:123
  319.5 3.2 fusion.21
  328.8 2.2 convolution_convert_fusion
  331.0 2.3 convolution_convert_fusion.1
  334.3 2.6 fusion.68
  341.9 88.6 %all-reduce.7.cloned.1.call-done = (bf16[2,1536,256]{1,2,0:T(8,128)(2,1)}, bf16[2,1536,256]{1,2,0:T(8,128)(2,1)}, bf16[2,256,1536]{2,1,0:T(8,128)(2,1)}) async-done(((bf16[2,1536,256]{1,2,0:T(8,128)(2,1)}, bf16[2,1536,256]{1,2,0:T(8,128)(2,1)}, bf16[2,256,1536]{2,1,0:T(8,128)(2,1)}), (bf16[2,1536,256]{1,2,0:T(8,128)(2,1)}, bf16[2,1536,256]{1,2,0:T(8,128)(2,1)}, ...) | async-done | bytes 4718608 | tf_op jit(solution)/shard_map/psum | solution.py:130
  430.5 3.1 copy.95
  433.6 3.1 copy.96
  436.7 3.6 convert_element_type.191
  442.9 40.8 %psum.56 = f32[2,1536]{1,0:T(2,128)} all-reduce(f32[2,1536]{1,0:T(2,128)} %pad_maximum_fusion.15), channel_id=1, replica_groups=mesh['dp'=2,'expert'=8,'tensor'=2] {'dp','expert','tensor'}, use_global_device_ids=true, to_apply=%region_13.14 | all-reduce | flops 3072 | bytes 24576 | tf_op jit(solution)/shard_map/psum | solution.py:171
  486.4 24.1 %reduce-scatter.3.cloned.1.call-done = bf16[128,1536]{1,0:T(8,128)(2,1)} async-done(((bf16[1024,1536]{1,0:T(8,128)(2,1)}), bf16[128,1536]{1,0:T(8,128)(2,1)}) %reduce-scatter.3.cloned.1.call-update) | async-done | bytes 393232 | tf_op jit(solution)/shard_map/reduce_scatter | solution.py:124
  510.6 3.3 subtract_add_fusion
  513.9 216.3 %all-reduce.5.cloned.1.call-done = (bf16[1536,768]{1,0:T(8,128)(2,1)}, bf16[1536,256]{1,0:T(8,128)(2,1)}, bf16[1536,256]{1,0:T(8,128)(2,1)}, bf16[768,1536]{1,0:T(8,128)(2,1)}) async-done(((bf16[1536,768]{1,0:T(8,128)(2,1)}, bf16[1536,256]{1,0:T(8,128)(2,1)}, bf16[1536,256]{1,0:T(8,128)(2,1)}, bf16[768,1536]{1,0:T(8,128)(2,1)}), (bf16[1536,768]{1,0:T(8,128)(2,1)}, bf16[1536,256]{1,0:T(8,128)(2,1)}, ...) | async-done | bytes 6291472 | tf_op jit(solution)/shard_map/psum | solution.py:170
  730.2 2.5 convert_element_type.178
  734.0 2.5 convert_element_type.176
  736.6 2.8 convert_element_type.182
  (230 shorter events, 65.7 us)
Async XLA Ops:
  7.2 13.0 %copy-start = (bf16[768,1536]{1,0:T(8,128)(2,1)S(1)}, bf16[768,1536]{1,0:T(8,128)(2,1)}, u32[]{:S(2)}) copy-start(bf16[768,1536]{1,0:T(8,128)(2,1)} %param.23) | copy-start | bytes 7077892
  7.2 7.1 copy-start.14
  7.2 7.1 copy-start.47
  7.2 81.2 %all-gather.5.cloned.1.call-start = ((), (), s32[]{:S(2)}) async-start(), calls=%async_computation.3 | async-start | bytes 3538944 | tf_op jit(solution)/shard_map/all_gather | solution.py:108
  7.3 3.8 collective-permute-start
  7.8 6.6 copy-start.11
  10.2 9.1 %copy-start.42 = (pred[256,256]{0,1:T(8,128)(4,1)}, pred[256,256]{0,1:T(8,128)(4,1)S(1)}, u32[]{:S(2)}) copy-start(pred[256,256]{0,1:T(8,128)(4,1)S(1)} %compare_and_fusion) | copy-start | bytes 196612
  11.0 10.1 %copy-start.16 = (bf16[128,1536]{1,0:T(8,128)(2,1)}, bf16[128,1536]{1,0:T(8,128)(2,1)S(1)}, u32[]{:S(2)}) copy-start(bf16[128,1536]{1,0:T(8,128)(2,1)S(1)} %collective-permute-done) | copy-start | bytes 1179652
  21.1 2.4 collective-permute-start.1
  25.6 169.8 %all-gather.3.cloned.1.call-start = ((), (), s32[]{:S(2)}) async-start(), calls=%async_computation.2 | async-start | bytes 7667712 | tf_op jit(solution)/shard_map/all_gather | solution.py:83
  30.0 279.0 %reduce-scatter.5.cloned.1.call-start = ((), (), s32[]{:S(2)}) async-start(), calls=%async_computation.5 | async-start | bytes 3538944 | tf_op jit(solution)/shard_map/reduce_scatter | solution.py:123
  30.5 8.6 %collective-permute-start.4 = (bf16[2,256,1536]{2,1,0:T(8,128)(2,1)}, bf16[2,256,1536]{2,1,0:T(8,128)(2,1)}, u32[]{:S(2)}, u32[]{:S(2)}) collective-permute-start(bf16[2,256,1536]{2,1,0:T(8,128)(2,1)} %param.26), channel_id=1, source_target_pairs={{0,1},{1,0},{2,3},{3,2},{4,5},{5,4},{6,7},{7,6},{8,9},{9,8},{10,11... | collective-permute-start | bytes 4718600 | tf_op jit(solution)/shard_map/ppermute | solution.py:16
  33.3 8.5 %collective-permute-start.3 = (bf16[2,1536,256]{1,2,0:T(8,128)(2,1)}, bf16[2,1536,256]{1,2,0:T(8,128)(2,1)}, u32[]{:S(2)}, u32[]{:S(2)}) collective-permute-start(bf16[2,1536,256]{1,2,0:T(8,128)(2,1)} %copy.83), channel_id=1, source_target_pairs={{0,1},{1,0},{2,3},{3,2},{4,5},{5,4},{6,7},{7,6},{8,9},{9,8},{10,11... | collective-permute-start | bytes 4718600 | tf_op jit(solution)/shard_map/ppermute | solution.py:16
  36.2 60.7 %collective-permute-start.2 = (bf16[2,1536,256]{1,2,0:T(8,128)(2,1)}, bf16[2,1536,256]{1,2,0:T(8,128)(2,1)}, u32[]{:S(2)}, u32[]{:S(2)}) collective-permute-start(bf16[2,1536,256]{1,2,0:T(8,128)(2,1)} %copy.81), channel_id=1, source_target_pairs={{0,1},{1,0},{2,3},{3,2},{4,5},{5,4},{6,7},{7,6},{8,9},{9,8},{10,11... | collective-permute-start | bytes 4718600 | tf_op jit(solution)/shard_map/ppermute | solution.py:16
  88.4 8.4 %copy-start.13 = (bf16[2,1536,256]{1,2,0:T(8,128)(2,1)S(1)}, bf16[2,1536,256]{1,2,0:T(8,128)(2,1)}, u32[]{:S(2)}) copy-start(bf16[2,1536,256]{1,2,0:T(8,128)(2,1)} %copy.81) | copy-start | bytes 4718596
  88.4 8.4 %copy-start.60 = (bf16[1024,1536]{1,0:T(8,128)(2,1)S(1)}, bf16[1024,1536]{1,0:T(8,128)(2,1)}, u32[]{:S(2)}) copy-start(bf16[1024,1536]{1,0:T(8,128)(2,1)} %all-gather.5.cloned.1.call-done) | copy-start | bytes 9437188
  202.7 11.6 %copy-start.1 = (f32[1024,1536]{1,0:T(8,128)}, f32[1024,1536]{1,0:T(8,128)S(1)}, u32[]{:S(2)}) copy-start(f32[1024,1536]{1,0:T(8,128)S(1)} %split.72) | copy-start | bytes 18874372
  202.7 11.7 %copy-start.12 = (bf16[2,1536,256]{1,2,0:T(8,128)(2,1)S(1)}, bf16[2,1536,256]{1,2,0:T(8,128)(2,1)}, u32[]{:S(2)}) copy-start(bf16[2,1536,256]{1,2,0:T(8,128)(2,1)} %copy.83) | copy-start | bytes 4718596
  214.4 8.8 %copy-start.63 = (bf16[2,1024,512]{1,2,0:T(8,128)(2,1)}, bf16[2,1024,512]{1,2,0:T(8,128)(2,1)S(1)}, u32[]{:S(2)}) copy-start(bf16[2,1024,512]{1,2,0:T(8,128)(2,1)S(1)} %get-tuple-element.61) | copy-start | bytes 6291460
  236.2 194.3 %all-reduce.7.cloned.1.call-start = ((), (), s32[]{:S(2)}) async-start(), calls=%async_computation.7 | async-start | bytes 9437184 | tf_op jit(solution)/shard_map/psum | solution.py:130
  236.5 7.4 copy-start.65
  243.8 10.4 %collective-permute-start.9 = (bf16[2,256,1536]{2,1,0:T(8,128)(2,1)S(1)}, bf16[2,256,1536]{2,1,0:T(8,128)(2,1)S(1)}, u32[]{:S(2)}, u32[]{:S(2)}) collective-permute-start(bf16[2,256,1536]{2,1,0:T(8,128)(2,1)S(1)} %split.111), channel_id=1, source_target_pairs={{0,1},{1,0},{2,3},{3,2},{4,5},{5,4},{6,7},{7,6},{8,9},{9,8},{10,11... | collective-permute-start | bytes 4718600 | tf_op jit(solution)/shard_map/ppermute | solution.py:16
  249.1 6.7 collective-permute-start.7
  254.1 3.5 collective-permute-start.8
  259.2 251.4 %reduce-scatter.3.cloned.1.call-start = ((), (), s32[]{:S(2)}) async-start(), calls=%async_computation.4 | async-start | bytes 3538944 | tf_op jit(solution)/shard_map/reduce_scatter | solution.py:124
  268.4 40.7 %copy-start.53 = (f32[128]{0:T(128)S(1)}, f32[128]{0:T(128)}, u32[]{:S(2)}) copy-start(f32[128]{0:T(128)} %copy-done.52) | copy-start | bytes 1540
  268.4 42.5 %copy-start.55 = (f32[128]{0:T(128)S(1)}, f32[128]{0:T(128)}, u32[]{:S(2)}) copy-start(f32[128]{0:T(128)} %get-tuple-element.79) | copy-start | bytes 1540
  268.4 461.8 %all-reduce.5.cloned.1.call-start = ((), (), s32[]{:S(2)}) async-start(), calls=%async_computation.6 | async-start | bytes 12582912 | tf_op jit(solution)/shard_map/psum | solution.py:170
  312.3 1.8 collective-permute-start.5
  324.2 6.7 copy-start.19
  340.6 99.8 %collective-permute-start.6 = (f32[128,1536]{1,0:T(8,128)}, f32[128,1536]{1,0:T(8,128)}, u32[]{:S(2)}, u32[]{:S(2)}) collective-permute-start(f32[128,1536]{1,0:T(8,128)} %slice.53), channel_id=1, source_target_pairs={{0,1},{1,0},{2,3},{3,2},{4,5},{5,4},{6,7},{7,6},{8,9},{9,8},{10,11... | collective-permute-start | bytes 2359304 | tf_op jit(solution)/shard_map/ppermute | solution.py:16
  440.3 70.2 %copy-start.6 = (bf16[128,1536]{1,0:T(8,128)(2,1)S(1)}, bf16[128,1536]{1,0:T(8,128)(2,1)}, u32[]{:S(2)}) copy-start(bf16[128,1536]{1,0:T(8,128)(2,1)} %param.27) | copy-start | bytes 1179652
  (51 other events, 112.5 us)
Sparse Core Ops, SparseCore 0:
  25.7 62.6 all-gather.4
  91.2 104.1 all-gather.2
  236.3 72.6 reduce-scatter.4
  311.5 119.0 all-reduce.6
  435.0 75.5 reduce-scatter.2
  518.5 211.5 all-reduce.4
